TPU v7x, 512 devices: a whole 4x4x16 slice. The times are simulated.
512 devices in a mesh: gx: 32 (over y, z_lo, core), gy: 16 (over x, z_hi).
Axes of the slice: x: 4, y: 4, z: 16 (z_hi: 4, z_lo: 4; z = z_hi * 4 + z_lo), core: 2. Of those that a mesh axis runs over, the one named last changes fastest.
Arguments:
- tokens: bfloat16 [2, 16, 128, 128, 512], P(None, None, 'gx', 'gy'), may hold values from -6 to 6
- norm_gain: float32 [512], replicated, may hold values from 0.1 to 1.9
- w_qkv: bfloat16 [512, 1536], replicated, may hold values from -12 to 12
- w_out: bfloat16 [512, 512], replicated, may hold values from -1 to 1
Outputs:
- result: bfloat16 [2, 16, 128, 128, 512], P(None, None, 'gx', 'gy')
All inputs are finite; a program needn't handle non-finite values.
Results may differ from a plain program's by a relative error of at most 0.0095.
Values may be sent and summed in bfloat16 or wider, within the bound.
A program may use at most 64 MiB of HBM per device.

v0:
```python
import jax
import jax.numpy as jnp
from jax import lax
from jax.sharding import PartitionSpec as P

HEADS = 8


def attend(triple, seq_dim):
    shape = triple.shape
    width = shape[-1] // 3
    head_size = width // HEADS
    split = shape[:-1] + (HEADS, head_size)
    queries = triple[..., :width].reshape(split)
    key_part = triple[..., width : 2 * width].reshape(split)
    values = triple[..., 2 * width :].reshape(split)
    if seq_dim == 1:
        form_scores, form_mix = ("asche,atche->achst", "achst,atche->asche")
    else:
        form_scores, form_mix = ("acshe,acthe->achst", "achst,acthe->acshe")
    scores = jnp.einsum(
        form_scores, queries, key_part, preferred_element_type=jnp.float32
    ) / jnp.sqrt(jnp.float32(head_size))
    highest = jnp.max(scores, axis=-1, keepdims=True)
    expo = jnp.exp(scores - highest)
    weights = (expo / jnp.sum(expo, axis=-1, keepdims=True)).astype(jnp.bfloat16)
    mixed = jnp.einsum(form_mix, weights, values, preferred_element_type=jnp.float32)
    return mixed.reshape(shape[:-1] + (width,)).astype(jnp.bfloat16)


def project(normed, w_qkv):
    width = normed.shape[-1]
    flat = jnp.dot(normed.reshape(-1, width), w_qkv, preferred_element_type=jnp.float32).astype(
        jnp.bfloat16
    )
    return flat.reshape(normed.shape[:-1] + (3 * width,))


def body(tokens, norm_gain, w_qkv, w_out):
    batch, steps, cells_x, cells_y, width = tokens.shape
    field = tokens.astype(jnp.float32)
    normed = (
        field * lax.rsqrt(jnp.mean(field * field, axis=-1, keepdims=True) + 1e-05) * norm_gain
    ).astype(jnp.bfloat16)
    triple = project(normed, w_qkv)
    along_time = attend(triple.reshape(batch, steps, cells_x * cells_y, 3 * width), 1)
    along_time = along_time.reshape(batch, steps, cells_x, cells_y, width)
    line_rows = batch * steps
    outgoing = triple.reshape(line_rows, cells_x, cells_y, 3 * width)
    outcome = attend(lax.all_to_all(outgoing, "gx", split_axis=0, concat_axis=1, tiled=True), 1)
    along_x = lax.all_to_all(outcome, "gx", split_axis=1, concat_axis=0, tiled=True)
    outcome = attend(lax.all_to_all(outgoing, "gy", split_axis=0, concat_axis=2, tiled=True), 2)
    along_y = lax.all_to_all(outcome, "gy", split_axis=2, concat_axis=0, tiled=True)
    mixed = (
        along_time.astype(jnp.float32)
        + along_x.reshape(along_time.shape).astype(jnp.float32)
        + along_y.reshape(along_time.shape).astype(jnp.float32)
    ).astype(jnp.bfloat16)
    update = jnp.dot(mixed.reshape(-1, width), w_out, preferred_element_type=jnp.float32)
    return (field + update.reshape(field.shape)).astype(jnp.bfloat16)


def solution(mesh):
    placed = (P(None, None, "gx", "gy", None), P(), P(), P())
    return jax.shard_map(
        body, mesh=mesh, in_specs=placed, out_specs=P(None, None, "gx", "gy", None), check_vma=False
    )
```

profile of v0, /device:TPU:1, one launch (start us, length us, event | category | flops | bytes accessed | tf_op | source)
XLA Modules:
  0.0 368.7 jit_solution(13969389955353461262)
XLA Ops:
  0.0 1.6 fusion.12
  3.2 1.8 convolution_convert_fusion
  5.0 1.7 copy-done.2
  6.7 159.2 %all_to_all.48 = bf16[32,4,8,1536]{3,2,1,0:T(8,128)(2,1)} all-to-all(bf16[32,4,8,1536]{3,2,1,0:T(8,128)(2,1)S(1)} %bitcast.63), channel_id=1, replica_groups=mesh['gx'=32,'gy'=16] {'gy'}, dimensions={0} | all-to-all | bytes 6291456 | tf_op jit(solution)/shard_map/all_to_all | solution.py:52
  165.9 8.9 %all-to-all-start = ((bf16[32,4,8,1536]{3,2,1,0:T(8,128)(2,1)}), bf16[32,4,8,1536]{3,2,1,0:T(8,128)(2,1)}, u32[]{:S(2)}, u32[]{:S(2)}) async-start(bf16[32,4,8,1536]{3,2,1,0:T(8,128)(2,1)} %bitcast.64), calls=%async_computation | async-start | bytes 6291456 | tf_op jit(solution)/shard_map/all_to_all | solution.py:50
  174.9 2.2 copy.82
  178.4 2.3 copy.59
  182.6 5.1 %fusion.47 = (f32[2,4,8,128]{3,2,1,0:T(8,128)S(1)}, f32[2,4,8,128,128]{3,4,2,1,0:T(8,128)}) fusion(bf16[2,4,128,8,64]{2,4,3,1,0:T(8,128)(2,1)} %bitcast.70, bf16[2,4,128,8,64]{2,4,3,1,0:T(8,128)(2,1)} %bitcast.72), kind=kOutput, calls=%fused_computation.54 | convolution fusion | flops 137363584 | bytes 6324224 | tf_op jit(solution)/shard_map/sub | solution.py:25
  187.7 2.9 fusion.31
  190.6 1.7 copy.62
  192.3 54.6 %all-to-all-done = bf16[32,4,8,1536]{3,2,1,0:T(8,128)(2,1)} async-done(((bf16[32,4,8,1536]{3,2,1,0:T(8,128)(2,1)}), bf16[32,4,8,1536]{3,2,1,0:T(8,128)(2,1)}, u32[]{:S(2)}, u32[]{:S(2)}) %all-to-all-start) | async-done | bytes 3145760 | tf_op jit(solution)/shard_map/all_to_all | solution.py:50
  246.9 7.5 %all-to-all-start.3 = ((bf16[2,4,128,512]{3,1,0,2:T(4,128)(2,1)}), bf16[2,4,128,512]{3,1,0,2:T(4,128)(2,1)S(1)}, u32[]{:S(2)}, u32[]{:S(2)}) async-start(bf16[2,4,128,512]{3,1,0,2:T(4,128)(2,1)} %copy.62), calls=%async_computation.3 | async-start | bytes 2097152 | tf_op jit(solution)/shard_map/all_to_all | solution.py:53
  254.4 3.4 fusion.43
  257.8 2.7 copy.70
  260.5 2.7 copy.71
  263.2 1.7 copy.69
  264.9 5.2 %fusion.46 = (f32[8,8,128]{2,1,0:T(8,128)S(1)}, f32[8,8,128,128]{2,3,1,0:T(8,128)}) fusion(bf16[128,8,8,64]{0,3,2,1:T(8,128)(2,1)} %bitcast.71, bf16[128,8,8,64]{0,3,2,1:T(8,128)(2,1)} %bitcast.74), kind=kOutput, calls=%fused_computation.53 | convolution fusion | flops 137363584 | bytes 6324224 | tf_op jit(solution)/shard_map/sub | solution.py:25
  270.1 3.9 %fusion.32 = bf16[8,8,64,128]{3,2,1,0:T(8,128)(2,1)} fusion(bf16[128,8,8,64]{0,3,2,1:T(8,128)(2,1)S(1)} %bitcast.75, f32[8,8,128,128]{2,3,1,0:T(8,128)} %get-tuple-element.17, f32[8,8,128]{2,1,0:T(8,128)S(1)} %get-tuple-element.16), kind=kOutput, calls=%fused_computation.41 | convolution fusion | flops 136839168 | bytes 6324224 | tf_op jit(solution)/shard_map/achst,atche->asche/dot_general | solution.py:27
  273.9 2.7 copy.56
  276.6 29.7 %all-to-all-done.3 = bf16[2,4,128,512]{3,1,0,2:T(4,128)(2,1)S(1)} async-done(((bf16[2,4,128,512]{3,1,0,2:T(4,128)(2,1)}), bf16[2,4,128,512]{3,1,0,2:T(4,128)(2,1)S(1)}, u32[]{:S(2)}, u32[]{:S(2)}) %all-to-all-start.3) | async-done | bytes 1048608 | tf_op jit(solution)/shard_map/all_to_all | solution.py:53
  306.4 10.5 %all-to-all-start.1 = ((bf16[1,128,8,512]{3,2,0,1:T(8,128)(2,1)}), bf16[1,128,8,512]{3,2,0,1:T(8,128)(2,1)}, u32[]{:S(2)}, u32[]{:S(2)}) async-start(bf16[1,128,8,512]{3,2,0,1:T(8,128)(2,1)} %copy.56), calls=%async_computation.1 | async-start | bytes 2097152 | tf_op jit(solution)/shard_map/all_to_all | solution.py:51
  316.8 3.6 fusion.44
  320.4 3.9 %reshape.118 = bf16[2,16,32,8,64]{4,3,2,1,0:T(8,128)(2,1)} reshape(bf16[2,16,32,512]{3,2,1,0:T(8,128)(2,1)} %get-tuple-element.13) | data formatting | bytes 2097152 | tf_op jit(solution)/shard_map/reshape | solution.py:14
  324.3 3.9 %reshape.119 = bf16[2,16,32,8,64]{4,3,2,1,0:T(8,128)(2,1)} reshape(bf16[2,16,32,512]{3,2,1,0:T(8,128)(2,1)} %get-tuple-element.12) | data formatting | bytes 2097152 | tf_op jit(solution)/shard_map/reshape | solution.py:15
  328.2 2.1 reshape.117
  330.3 4.7 %fusion.20 = f32[2,32,8,16,16]{3,4,2,1,0:T(8,128)S(1)} fusion(bf16[2,16,32,8,64]{4,3,2,1,0:T(8,128)(2,1)} %reshape.119, bf16[2,16,32,8,64]{4,3,2,1,0:T(8,128)(2,1)} %reshape.118), kind=kOutput, calls=%fused_computation.31 | convolution fusion | flops 16777216 | bytes 2621440 | tf_op jit(solution)/shard_map/asche,atche->achst/dot_general | solution.py:21
  335.0 17.7 %fusion.45 = (f32[2,32,8,16]{3,2,1,0:T(8,128)S(1)}, f32[2,32,8,16,16]{3,4,2,1,0:T(8,128)S(1)}) fusion(f32[2,32,8,16,16]{3,4,2,1,0:T(8,128)S(1)} %fusion.20), kind=kOutput, calls=%fused_computation.52 | output fusion | flops 524303 | bytes 1081344 | tf_op jit(solution)/shard_map/sub | solution.py:25
  352.8 1.7 convert_bitcast_fusion
  354.5 3.2 copy.51
  357.6 4.8 %reshape.126 = f32[2,16,4,8,512]{4,3,2,1,0:T(8,128)} reshape(f32[2,16,32,8,64]{4,3,2,1,0:T(8,128)} %copy.51) | data formatting | bytes 4194304 | tf_op jit(solution)/shard_map/convert_element_type | solution.py:55
  362.8 1.6 copy.64
  364.4 4.3 %fusion.15 = bf16[2,16,4,8,512]{4,3,2,1,0:T(8,128)(2,1)} fusion(bf16[2,16,4,8,512]{4,3,2,1,0:T(8,128)(2,1)S(1)} %copy-done.3, f32[2,16,4,8,512]{4,3,2,1,0:T(8,128)} %reshape.126, bf16[2,16,4,8,512]{4,3,2,1,0:T(8,128)(2,1)} %bitcast.27, bf16[512,512]{1,0:T(8,128)(2,1)S(1)} %copy-done.6, f32[2,16,4,8,512]{4,3,2,1,0:T(8,128)} %bitcast.68), kind=kOutput, calls=%fused_computation.24 | convolution fusion | flops 540540928 | bytes 7864320 | tf_op jit(solution)/shard_map/dot_general | solution.py:59
  (20 shorter events, 5.2 us)
Async XLA Ops:
  0.0 3.2 copy-start
  5.0 1.7 copy-start.2
  165.9 80.9 %all-to-all-start = ((bf16[32,4,8,1536]{3,2,1,0:T(8,128)(2,1)}), bf16[32,4,8,1536]{3,2,1,0:T(8,128)(2,1)}, u32[]{:S(2)}, u32[]{:S(2)}) async-start(bf16[32,4,8,1536]{3,2,1,0:T(8,128)(2,1)} %bitcast.64), calls=%async_computation | async-start | bytes 6291456 | tf_op jit(solution)/shard_map/all_to_all | solution.py:50
  246.9 59.5 %all-to-all-start.3 = ((bf16[2,4,128,512]{3,1,0,2:T(4,128)(2,1)}), bf16[2,4,128,512]{3,1,0,2:T(4,128)(2,1)S(1)}, u32[]{:S(2)}, u32[]{:S(2)}) async-start(bf16[2,4,128,512]{3,1,0,2:T(4,128)(2,1)} %copy.62), calls=%async_computation.3 | async-start | bytes 2097152 | tf_op jit(solution)/shard_map/all_to_all | solution.py:53
  264.9 5.2 %copy-start.5 = (bf16[1,128,8,512]{1,3,2,0:T(8,128)(2,1)S(1)}, bf16[1,128,8,512]{1,3,2,0:T(8,128)(2,1)}, u32[]{:S(2)}) copy-start(bf16[1,128,8,512]{1,3,2,0:T(8,128)(2,1)} %copy.69) | copy-start | bytes 3145732
  306.4 58.0 %all-to-all-start.1 = ((bf16[1,128,8,512]{3,2,0,1:T(8,128)(2,1)}), bf16[1,128,8,512]{3,2,0,1:T(8,128)(2,1)}, u32[]{:S(2)}, u32[]{:S(2)}) async-start(bf16[1,128,8,512]{3,2,0,1:T(8,128)(2,1)} %copy.56), calls=%async_computation.1 | async-start | bytes 2097152 | tf_op jit(solution)/shard_map/all_to_all | solution.py:51
  335.0 17.7 %copy-start.4 = (bf16[2,16,32,8,64]{4,3,2,1,0:T(8,128)(2,1)S(1)}, bf16[2,16,32,8,64]{4,3,2,1,0:T(8,128)(2,1)}, u32[]{:S(2)}) copy-start(bf16[2,16,32,8,64]{4,3,2,1,0:T(8,128)(2,1)} %reshape.117) | copy-start | bytes 3145732
  362.4 1.9 copy-start.3
  362.4 1.9 copy-start.6
  364.4 4.4 %copy-start.1 = (bf16[512,1536]{1,0:T(8,128)(2,1)S(1)}, bf16[512,1536]{1,0:T(8,128)(2,1)}, u32[]{:S(2)}) copy-start(bf16[512,1536]{1,0:T(8,128)(2,1)} %param.6) | copy-start | bytes 4718596
where the time goes:
time: 370 us; the launch traced here: 369 us
  blocking collectives  159 us (43%)
  waiting for transfers between devices  84.3 us (23%)
  local copies, waits for them, and re-layouts  47.3 us (13%)
  matrix products  29.6 us (8%)
  starting transfers between devices  26.9 us (7%)
  other arithmetic  21.3 us (6%)
    all_to_all x1, blocking collectives, body(): lax.all_to_all(outgoing, 'gy', split_axis=0, concat_axis=2, tiled=True)  159 us
    all_to_all x1, waiting for transfers between devices, body(): lax.all_to_all(outgoing, 'gx', split_axis=0, concat_axis=1, tiled=True)  54.6 us
    all_to_all x1, waiting for transfers between devices, body(): lax.all_to_all(outcome, 'gy', split_axis=2, concat_axis=0, tiled=True)  29.7 us
    sub x1, other arithmetic, attend(): expo = jnp.exp(scores - highest)  17.7 us
    all_to_all x1, starting transfers between devices, body(): lax.all_to_all(outcome, 'gx', split_axis=1, concat_axis=0, tiled=True)  10.5 us
    sub x2, matrix products, attend(): expo = jnp.exp(scores - highest)  10.3 us
    all_to_all x1, starting transfers between devices, body(): lax.all_to_all(outgoing, 'gx', split_axis=0, concat_axis=1, tiled=True)  8.91 us
    unnamed x17, local copies, waits for them, and re-layouts  8.72 us
  transfers between devices with their start and end apart: 3, of which 2 were waited for; matrix products, arithmetic and copies ran while one was open for 24% of the time, Pallas kernels for 0%

commit v1 on v0

v1 whole, which is shorter than its diff:
```python
import functools

import jax
import jax.numpy as jnp
from jax import lax
from jax.experimental import pallas as pl
from jax.experimental.pallas import tpu as pltpu
from jax.sharding import PartitionSpec as P

NZ = 16
ROWS = 32
D = 512
MESH = pl.DeviceIdType.MESH
BF = jnp.bfloat16
F32 = jnp.float32


def device(y, zl, core, x, zh):
    return ((y * 4 + zl) * 2 + core, x * 4 + zh)


def kernel(
    tok, gain, wq, wo, out,
    t_s, xn, r1, ry, rx, oy, ox, by, bx, sm, h, tm, res, qkv, of, w, wos,
    load_sem, loc_sem, zs, zr, ys, yr, xs, xr, bys, byr, bxs, bxr, rs, rr, out_sem,
):
    gx, gy = lax.axis_index("gx"), lax.axis_index("gy")
    y, zl, core = gx // 8, (gx // 2) % 4, gx % 2
    x, zh = gy // 4, gy % 4
    z = zh * 4 + zl
    yc = y * 2 + core

    loads = [
        pltpu.make_async_copy(tok.at[0], t_s.at[0], load_sem.at[0]),
        pltpu.make_async_copy(tok.at[1], t_s.at[1], load_sem.at[1]),
        pltpu.make_async_copy(wq, w, load_sem.at[2]),
        pltpu.make_async_copy(wo, wos, load_sem.at[3]),
    ]
    for copy in loads:
        copy.start()

    barrier = pltpu.get_barrier_semaphore()

    def z_peer(i):
        other = (z + i) % NZ
        return other, device(y, other % 4, core, x, other // 4)

    def x_peer(i):
        other = (x + i) % 4
        return other, device(y, zl, core, other, zh)

    def yc_peer(i):
        other = (yc + i) % 8
        return other, device(other // 2, zl, other % 2, x, zh)

    def greet(peer):
        def step(i, carry):
            pl.semaphore_signal(barrier, inc=1, device_id=peer(i)[1], device_id_type=MESH)
            return carry

        return step

    lax.fori_loop(1, NZ, greet(z_peer), 0)
    lax.fori_loop(1, 4, greet(x_peer), 0)
    lax.fori_loop(1, 8, greet(yc_peer), 0)

    scale = gain[...]

    def normalize(b):
        def step(i, carry):
            field = t_s[b, i].astype(F32)
            mean = jnp.mean(field * field, axis=-1, keepdims=True)
            xn[b, i] = (field * lax.rsqrt(mean + 1e-05) * scale).astype(BF)
            return carry

        lax.fori_loop(0, NZ, step, 0)

    def send(src, dst, ssem, rsem, peer):
        pltpu.make_async_remote_copy(
            src_ref=src, dst_ref=dst, send_sem=ssem, recv_sem=rsem, device_id=peer, device_id_type=MESH
        ).start()

    def arrived(ref, sem):
        pltpu.make_async_copy(ref, ref, sem).wait()

    def forward(b):
        own = pltpu.make_async_copy(xn.at[b, z], r1.at[b, zh, zl], loc_sem.at[b, 0])
        own.start()

        def step(i, carry):
            other, peer = z_peer(i)
            send(xn.at[b, other], r1.at[b, zh, zl], zs.at[b], zr.at[b], peer)
            return carry

        lax.fori_loop(1, NZ, step, 0)

    def spread(b):
        arrived(xn.at[b, pl.ds(0, NZ - 1)], zr.at[b])
        pltpu.make_async_copy(xn.at[b, z], r1.at[b, zh, zl], loc_sem.at[b, 0]).wait()
        own = pltpu.make_async_copy(r1.at[b, :, x], ry.at[b, x], loc_sem.at[b, 1])
        own.start()

        def step(i, carry):
            other, peer = x_peer(i)
            send(r1.at[b, :, other], ry.at[b, x], ys.at[b], yr.at[b], peer)
            return carry

        lax.fori_loop(1, 4, step, 0)

        @pl.when(core == b)
        def _():
            pltpu.make_async_copy(r1.at[b, y], rx.at[yc], loc_sem.at[b, 2]).start()

        def step_x(i, carry):
            other = (y + i) % 4

            @pl.when((other != y) | (core != b))
            def _():
                send(r1.at[b, other], rx.at[yc], xs.at[b], xr.at[b], device(other, zl, b, x, zh))

            return carry

        lax.fori_loop(0, 4, step_x, 0)

    def project(src, rows):
        def step(i, carry):
            at = pl.multiple_of(i * 256, 256)
            part = jnp.dot(src[...].reshape(rows, D), w[:, pl.ds(at, 256)], preferred_element_type=F32)
            qkv[2 * i, pl.ds(0, rows)] = part[:, :128]
            qkv[2 * i + 1, pl.ds(0, rows)] = part[:, 128:]
            return carry

        lax.fori_loop(0, 6, step, 0)

    low = lax.broadcasted_iota(jnp.int32, (128, 128), 1) < 64
    ones = jnp.ones((128, 128), BF)

    def line(load, store, mask):
        for pair in range(4):
            q = load(pair) * 0.125
            k = load(4 + pair).astype(BF)
            v = load(8 + pair).astype(BF)
            both = jnp.concatenate([jnp.where(low, q, 0.0), jnp.where(low, 0.0, q)], axis=0).astype(BF)
            scores = lax.dot_general(both, k, (((1,), (1,)), ((), ())), preferred_element_type=F32)
            if mask is not None:
                scores = jnp.where(mask, scores, -3e38)
            weights = jnp.exp(scores - jnp.max(scores, axis=-1, keepdims=True)).astype(BF)
            total = jnp.dot(weights, jnp.concatenate([v, ones], axis=1), preferred_element_type=F32)
            part = jnp.where(low, total[:128, :128], total[128:, :128])
            norm = jnp.where(low, total[:128, 128:], total[128:, 128:])
            store(pair, part / norm)

    def aligned_lines(mask):
        def step(c, carry):
            def rows(g):
                return pl.ds(pl.multiple_of(g * ROWS + c * 8, 8), 8)

            def load(col):
                return jnp.concatenate([qkv[col, rows(g)] for g in range(16)], axis=0)

            def store(col, value):
                for g in range(16):
                    of[col, rows(g)] = value[8 * g : 8 * g + 8]

            line(load, store, mask)
            return carry

        lax.fori_loop(0, 4, step, 0)

    def strided_lines():
        def step(c, carry):
            def load(col):
                return qkv[col, pl.ds(c, 128, stride=8)]

            def store(col, value):
                of[col, pl.ds(c, 128, stride=8)] = value

            line(load, store, None)
            return carry

        lax.fori_loop(0, 8, step, 0)

    def rounded(dst, lead):
        def step(i, carry):
            at = pl.multiple_of(i * 128, 128)
            whole = jnp.concatenate([of[pair, pl.ds(at, 128)] for pair in range(4)], axis=1)
            dst[i] = whole.reshape(4, ROWS, D).astype(BF)
            return carry

        lax.fori_loop(0, lead, step, 0)

    row = lax.broadcasted_iota(jnp.int32, (256, 128), 0)
    column = lax.broadcasted_iota(jnp.int32, (256, 128), 1)
    same_cell = (row % 8) == (column % 8)

    def time_lines(b):
        project(xn.at[b], 512)
        aligned_lines(same_cell)
        rounded(tm.at[b], 4)

    def y_lines(b):
        arrived(ry.at[b, pl.ds(0, 3)], yr.at[b])
        pltpu.make_async_copy(r1.at[b, :, x], ry.at[b, x], loc_sem.at[b, 1]).wait()
        project(ry.at[b], 512)
        aligned_lines(None)
        rounded(oy.at[b], 4)
        pltpu.make_async_copy(oy.at[b, x], by.at[b, x], loc_sem.at[b, 3]).start()

        def step(i, carry):
            other, peer = x_peer(i)
            send(oy.at[b, other], by.at[b, x], bys.at[b], byr.at[b], peer)
            return carry

        lax.fori_loop(1, 4, step, 0)

    def x_lines(b):
        @pl.when(core == b)
        def _():
            arrived(rx.at[pl.ds(0, 7)], xr.at[b])
            pltpu.make_async_copy(r1.at[b, y], rx.at[yc], loc_sem.at[b, 2]).wait()
            project(rx, 1024)
            strided_lines()
            rounded(ox, 8)
            pltpu.make_async_copy(ox.at[yc], bx.at[b, y], loc_sem.at[b, 4]).start()

            def step(i, carry):
                other, peer = yc_peer(i)
                send(ox.at[other], bx.at[b, y], bxs.at[b], bxr.at[b], peer)
                return carry

            lax.fori_loop(1, 8, step, 0)

    def back(b):
        arrived(by.at[b, pl.ds(0, 3)], byr.at[b])
        pltpu.make_async_copy(oy.at[b, x], by.at[b, x], loc_sem.at[b, 3]).wait()

        @pl.when(core == b)
        def _():
            arrived(bx.at[b, pl.ds(0, 3)], bxr.at[b])
            pltpu.make_async_copy(ox.at[yc], bx.at[b, y], loc_sem.at[b, 4]).wait()

        @pl.when(core != b)
        def _():
            arrived(bx.at[b], bxr.at[b])

        def add(i, carry):
            high, part = i // 4, i % 4
            sm[b, i] = (bx[b, high, part].astype(F32) + by[b, part, high].astype(F32)).astype(BF)
            return carry

        lax.fori_loop(0, NZ, add, 0)
        pltpu.make_async_copy(sm.at[b, z], h.at[b, z], loc_sem.at[b, 5]).start()

        def step(i, carry):
            other, peer = z_peer(i)
            send(sm.at[b, other], h.at[b, z], rs.at[b], rr.at[b], peer)
            return carry

        lax.fori_loop(1, NZ, step, 0)

    def finish(b):
        arrived(h.at[b, pl.ds(0, NZ - 1)], rr.at[b])
        pltpu.make_async_copy(sm.at[b, z], h.at[b, z], loc_sem.at[b, 5]).wait()

        def step(i, carry):
            four = pl.ds(i * 4, 4)
            mixed = (tm[b, i].astype(F32) + h[b, four].astype(F32)).astype(BF)
            update = jnp.dot(mixed.reshape(128, D), wos[...], preferred_element_type=F32)
            res[b, four] = (t_s[b, four].astype(F32) + update.reshape(4, ROWS, D)).astype(BF)
            return carry

        lax.fori_loop(0, 4, step, 0)
        pltpu.make_async_copy(res.at[b], out.at[b], out_sem.at[b]).start()

    loads[0].wait()
    normalize(0)
    pl.semaphore_wait(barrier, 25)
    forward(0)
    loads[1].wait()
    normalize(1)
    forward(1)
    loads[2].wait()
    time_lines(0)
    time_lines(1)
    for b in range(2):
        spread(b)
        y_lines(b)
        x_lines(b)
        back(b)
    loads[3].wait()
    finish(0)
    finish(1)
    for b in range(2):
        pltpu.make_async_copy(res.at[b], out.at[b], out_sem.at[b]).wait()
        arrived(xn.at[b, pl.ds(0, NZ - 1)], zs.at[b])
        arrived(ry.at[b, pl.ds(0, 3)], ys.at[b])
        arrived(by.at[b, pl.ds(0, 3)], bys.at[b])
        arrived(h.at[b, pl.ds(0, NZ - 1)], rs.at[b])

        @pl.when(core == b)
        def _():
            arrived(r1.at[b, pl.ds(0, 3)], xs.at[b])
            arrived(ox.at[pl.ds(0, 7)], bxs.at[b])

        @pl.when(core != b)
        def _():
            arrived(r1.at[b], xs.at[b])


def body(tokens, norm_gain, w_qkv, w_out):
    shape = tokens.shape
    dma = pltpu.SemaphoreType.DMA
    result = pl.pallas_call(
        kernel,
        out_shape=jax.ShapeDtypeStruct((2, NZ, ROWS, D), BF),
        in_specs=[
            pl.BlockSpec(memory_space=pl.ANY),
            pl.BlockSpec(memory_space=pltpu.VMEM),
            pl.BlockSpec(memory_space=pl.ANY),
            pl.BlockSpec(memory_space=pl.ANY),
        ],
        out_specs=pl.BlockSpec(memory_space=pl.ANY),
        scratch_shapes=[
            pltpu.VMEM((2, NZ, ROWS, D), BF),
            pltpu.VMEM((2, NZ, ROWS, D), BF),
            pltpu.VMEM((2, 4, 4, ROWS, D), BF),
            pltpu.VMEM((2, 4, 4, ROWS, D), BF),
            pltpu.VMEM((8, 4, ROWS, D), BF),
            pltpu.VMEM((2, 4, 4, ROWS, D), BF),
            pltpu.VMEM((8, 4, ROWS, D), BF),
            pltpu.VMEM((2, 4, 4, ROWS, D), BF),
            pltpu.VMEM((2, 4, 4, ROWS, D), BF),
            pltpu.VMEM((2, NZ, ROWS, D), BF),
            pltpu.VMEM((2, NZ, ROWS, D), BF),
            pltpu.VMEM((2, 4, 4, ROWS, D), BF),
            pltpu.VMEM((2, NZ, ROWS, D), BF),
            pltpu.VMEM((12, 1024, 128), F32),
            pltpu.VMEM((4, 1024, 128), F32),
            pltpu.VMEM((D, 3 * D), BF),
            pltpu.VMEM((D, D), BF),
            dma((4,)),
            dma((2, 6)),
        ]
        + [dma((2,))] * 13,
        compiler_params=pltpu.CompilerParams(
            collective_id=0, has_side_effects=True, vmem_limit_bytes=48 * 1024 * 1024
        ),
        name="axial",
    )(tokens.reshape(2, NZ, ROWS, D), norm_gain.reshape(1, D), w_qkv, w_out)
    return result.reshape(shape)


def solution(mesh):
    placed = (P(None, None, "gx", "gy", None), P(), P(), P())
    return jax.shard_map(
        body, mesh=mesh, in_specs=placed, out_specs=P(None, None, "gx", "gy", None), check_vma=False
    )
```

time: 370 us -> 142 us (0.38)
  blocking collectives: 159 us -> 0 us
  Pallas kernels: 0 us -> 137 us
  waiting for transfers between devices: 84.3 us -> 0 us
  local copies, waits for them, and re-layouts: 47.3 us -> 5.33 us
  matrix products: 29.6 us -> 0 us
  starting transfers between devices: 26.9 us -> 0 us
  other arithmetic: 21.3 us -> 0 us
    all_to_all x1 -> x0, blocking collectives: 159 us -> none  [body(): lax.all_to_all(outgoing, 'gy', split_axis=0, concat_axis=2, tiled=True)]
    pallas_call x0 -> x1, Pallas kernels: none -> 137 us  [body(): pl.pallas_call(kernel, out_shape=jax.ShapeDtypeStruct((2, NZ, ROWS, D), B...]
    all_to_all x3 -> x0, waiting for transfers between devices: 84.3 us -> none  [the longest x1 54.6 us: body(): lax.all_to_all(outgoing, 'gx', split_axis=0, concat_axis=1, tiled=True)]
    all_to_all x3 -> x0, starting transfers between devices: 26.9 us -> none  [the longest x1 10.5 us: body(): lax.all_to_all(outcome, 'gx', split_axis=1, concat_axis=0, tiled=True)]
    dot_general x6 -> x0, matrix products: 19.3 us -> none  [the longest x3 8.41 us: attend(): jnp.einsum(form_mix, weights, values, preferred_element_type=jnp.float32)]
    sub x1 -> x0, other arithmetic: 17.7 us -> none  [attend(): expo = jnp.exp(scores - highest)]
    convert_element_type x5 -> x0, local copies, waits for them, and re-layouts: 14 us -> none  [the longest x2 7.97 us: body(): along_time.astype(jnp.float32)]
    slice x6 -> x0, local copies, waits for them, and re-layouts: 12.5 us -> none  [the longest x3 6.02 us: attend(): key_part = triple[..., width:2 * width].reshape(split)]
  transfers between devices with their start and end apart: 3 -> 0, of which waited for: 2 -> 0; matrix products, arithmetic and copies ran while one was open for 24% -> 0% of each run, Pallas kernels for 0% -> 0%
where the time goes in v1:
time: 142 us
  Pallas kernels  137 us (96%)
  local copies, waits for them, and re-layouts  5.33 us (4%)
    pallas_call x1, Pallas kernels, body(): pl.pallas_call(kernel, out_shape=jax.ShapeDtypeStruct((2, NZ, ROWS, D), B...  137 us
    unnamed x9, local copies, waits for them, and re-layouts  5.33 us

profile of v1, /device:TPU:1, one launch (start us, length us, event | category | flops | bytes accessed | tf_op | source)
XLA Modules:
  0.0 142.0 jit_solution(7611517992604186141)
XLA Ops:
  0.0 0.0 copy-start
  0.0 1.4 copy-done
  1.4 0.0 copy-start.1
  1.4 1.2 copy-done.1
  2.6 0.0 copy-start.2
  2.6 1.0 copy-done.2
  3.7 0.0 copy-start.3
  3.7 0.7 copy-done.3
  4.4 136.7 %axial.1 = bf16[2,16,32,512]{3,2,1,0:T(8,128)(2,1)S(1)} custom-call(bf16[2,16,32,512]{3,2,1,0:T(8,128)(2,1)S(1)} %bitcast.4, f32[1,512]{1,0:T(1,128)S(1)} %bitcast.5, bf16[512,1536]{1,0:T(8,128)(2,1)S(1)} %copy-done, bf16[512,512]{1,0:T(8,128)(2,1)S(1)} %copy-done.2), custom_call_target="tpu_custom_call" | custom-call | tf_op jit(solution)/shard_map/axial/pallas_call | solution.py:313
  141.0 1.0 copy.6
Async XLA Ops:
  0.0 1.4 copy-start
  1.4 1.2 copy-start.1
  2.6 1.0 copy-start.2
  3.7 0.7 copy-start.3

commit v2 on v0

v2 whole, which is shorter than its diff:
```python
import jax
import jax.numpy as jnp
from jax import lax
from jax.experimental import pallas as pl
from jax.experimental.pallas import tpu as pltpu
from jax.sharding import PartitionSpec as P

NZ = 16
ROWS = 32
D = 512
MESH = pl.DeviceIdType.MESH
BF = jnp.bfloat16
F32 = jnp.float32


def device(y, zl, core, x, zh):
    return ((y * 4 + zl) * 2 + core, x * 4 + zh)


def kernel(
    tok, gain, wq, wo, out,
    t_s, xn, r1, ry, rx, oy, ox, by, bx, sm, h, tm, qkv, of, sc, wt, w, wos,
    load_sem, w_sem, loc_sem, zs, zr, ys, yr, xs, xr, bys, byr, bxs, bxr, rs, rr,
):
    gx, gy = lax.axis_index("gx"), lax.axis_index("gy")
    y, zl, core = gx // 8, (gx // 2) % 4, gx % 2
    x, zh = gy // 4, gy % 4
    z = zh * 4 + zl
    yc = y * 2 + core

    for b in range(2):
        pltpu.make_async_copy(tok.at[b], t_s.at[b], load_sem.at[b]).start()

    barrier = pltpu.get_barrier_semaphore()

    def z_peer(i):
        other = (z + (i % 2) * ((i + 1) // 2) + (1 - i % 2) * (NZ - i // 2)) % NZ
        return other, device(y, other % 4, core, x, other // 4)

    def x_peer(i):
        other = (x + i) % 4
        return other, device(y, zl, core, other, zh)

    def yc_peer(i):
        other = (yc + i) % 8
        return other, device(other // 2, zl, other % 2, x, zh)

    def each(first, last, step):
        def run(i, carry):
            step(i)
            return carry

        lax.fori_loop(first, last, run, 0)

    def greet(peer):
        return lambda i: pl.semaphore_signal(barrier, inc=1, device_id=peer(i)[1], device_id_type=MESH)

    each(1, NZ, greet(z_peer))
    each(1, 4, greet(x_peer))
    each(1, 8, greet(yc_peer))

    def weight_load(pair, kind):
        cols = pl.ds(pl.multiple_of(kind * D + pair * 128, 128), 128)
        return pltpu.make_async_copy(wq.at[:, cols], w.at[pair, kind], w_sem.at[pair, kind])

    out_load = pltpu.make_async_copy(wo, wos, load_sem.at[2])
    for pair in range(4):
        for kind in range(3):
            weight_load(pair, kind).start()
    out_load.start()

    scale = gain[...]

    def normalize(b):
        def step(i):
            two = pl.ds(i * 2, 2)
            field = t_s[b, two].astype(F32)
            mean = jnp.mean(field * field, axis=-1, keepdims=True)
            xn[b, two] = (field * lax.rsqrt(mean + 1e-05) * scale).astype(BF)

        each(0, NZ // 2, step)

    def send(src, dst, ssem, rsem, peer):
        pltpu.make_async_remote_copy(
            src_ref=src, dst_ref=dst, send_sem=ssem, recv_sem=rsem, device_id=peer, device_id_type=MESH
        ).start()

    def keep(src, dst):
        copy = pltpu.make_async_copy(src, dst, loc_sem)
        copy.start()
        copy.wait()

    def arrived(ref, sem):
        pltpu.make_async_copy(ref, ref, sem).wait()

    def forward(b):
        def step(i):
            other, peer = z_peer(i)
            send(xn.at[b, other], r1.at[b, z], zs.at[b], zr.at[b, z], peer)

        each(1, NZ, step)
        keep(xn.at[b, z], r1.at[b, z])

    def spread(b):
        def pass_on(other):
            high, low_part = other // 4, other % 4
            block = r1.at[b, other]

            @pl.when((high != y) | (core != b))
            def _():
                send(block, rx.at[yc, low_part], xs.at[b], xr.at[b], device(high, zl, b, x, zh))

            @pl.when(low_part != x)
            def _():
                send(block, ry.at[b, x, high], ys.at[b], yr.at[b], device(y, zl, core, low_part, zh))

            @pl.when((high == y) & (core == b))
            def _():
                keep(block, rx.at[yc, low_part])

            @pl.when(low_part == x)
            def _():
                keep(block, ry.at[b, x, high])

        def step(i):
            other, _ = z_peer(i)
            arrived(r1.at[b, other], zr.at[b, other])
            pass_on(other)

        pass_on(z)
        each(1, NZ, step)

    def project(src, pair, tiles):
        weights = jnp.concatenate([w[pair, kind] for kind in range(3)], axis=1)

        def step(i):
            rows = pl.ds(pl.multiple_of(i * 512, 512), 512)
            part = jnp.dot(src[pl.ds(i * 16, 16)].reshape(512, D), weights, preferred_element_type=F32)
            for kind in range(3):
                qkv[kind, rows] = part[:, 128 * kind : 128 * kind + 128]

        if tiles == 1:
            step(0)
        else:
            each(0, tiles, step)

    low = lax.broadcasted_iota(jnp.int32, (128, 128), 1) < 64
    ones = jnp.ones((128, 128), BF)

    def lines(units, mask):
        def first(slot, load, store):
            q = load(0) * 0.125
            k = load(1).astype(BF)
            both = jnp.concatenate([jnp.where(low, q, 0.0), jnp.where(low, 0.0, q)], axis=0).astype(BF)
            scores = lax.dot_general(both, k, (((1,), (1,)), ((), ())), preferred_element_type=F32)
            if mask is not None:
                scores = jnp.where(mask, scores, -3e38)
            sc[slot] = scores

        def second(slot, load, store):
            scores = sc[slot]
            wt[slot] = jnp.exp(scores - jnp.max(scores, axis=-1, keepdims=True)).astype(BF)

        def third(slot, load, store):
            v = load(2).astype(BF)
            total = jnp.dot(wt[slot], jnp.concatenate([v, ones], axis=1), preferred_element_type=F32)
            part = jnp.where(low, total[:128, :128], total[128:, :128])
            norm = jnp.where(low, total[:128, 128:], total[128:, 128:])
            store(part / norm)

        for u in range(len(units) + 2):
            if u < len(units):
                first(u, *units[u])
            if 1 <= u <= len(units):
                second(u - 1, *units[u - 1])
            if u >= 2:
                third(u - 2, *units[u - 2])

    def aligned(c):
        def rows(g):
            return pl.ds(g * ROWS + c * 8, 8)

        def load(kind):
            return jnp.concatenate([qkv[kind, rows(g)] for g in range(16)], axis=0)

        def store(value):
            for g in range(16):
                of[rows(g)] = value[8 * g : 8 * g + 8]

        return load, store

    def strided(c):
        def load(kind):
            return qkv[kind, pl.ds(c, 128, stride=8)]

        def store(value):
            of[pl.ds(c, 128, stride=8)] = value

        return load, store

    def rounded(dst, blocks):
        def step(i):
            rows = pl.ds(pl.multiple_of(i * 256, 256), 256)
            dst[pl.ds(i * 8, 8)] = of[rows].reshape(8, ROWS, 128).astype(BF)

        each(0, blocks // 8, step)

    row = lax.broadcasted_iota(jnp.int32, (256, 128), 0)
    column = lax.broadcasted_iota(jnp.int32, (256, 128), 1)
    same_cell = (row % 8) == (column % 8)

    def time_lines(b):
        def step(pair):
            project(xn.at[b], pair, 1)
            lines([aligned(c) for c in range(4)], same_cell)
            rounded(tm.at[b, pair], 16)

        each(0, 4, step)

    def attend(b):
        arrived(ry.at[b, pl.ds(0, 3)], yr.at[b])

        @pl.when(core == b)
        def _():
            arrived(rx.at[pl.ds(0, 7)], xr.at[b])

        def step(pair):
            @pl.when(core == b)
            def _():
                project(rx_rows, pair, 2)
                lines([strided(c) for c in range(8)], None)
                rounded(ox.at[pair], 32)

                def give(i):
                    other, peer = yc_peer(i)
                    send(ox.at[pair, pl.ds(other * 4, 4)], bx.at[b, pair, y], bxs.at[pair], bxr.at[b, pair], peer)

                each(1, 8, give)
                keep(ox.at[pair, pl.ds(yc * 4, 4)], bx.at[b, pair, y])

            project(ry_rows.at[b], pair, 1)
            lines([aligned(c) for c in range(4)], None)
            rounded(oy.at[b, pair], 16)

            def give(i):
                other, peer = x_peer(i)
                send(oy.at[b, pair, pl.ds(other * 4, 4)], by.at[b, pair, x], bys.at[b, pair], byr.at[b, pair], peer)

            each(1, 4, give)
            keep(oy.at[b, pair, pl.ds(x * 4, 4)], by.at[b, pair, x])

        each(0, 4, step)

    rx_rows = rx.reshape(32, ROWS, D)
    ry_rows = ry.reshape(2, 16, ROWS, D)

    def back(b):
        def step(pair):
            arrived(by.at[b, pair, pl.ds(0, 3)], byr.at[b, pair])

            @pl.when(core == b)
            def _():
                arrived(bx.at[b, pair, pl.ds(0, 3)], bxr.at[b, pair])

            @pl.when(core != b)
            def _():
                arrived(bx.at[b, pair], bxr.at[b, pair])

            for high in range(4):
                for part in range(4):
                    total = bx[b, pair, high, part].astype(F32) + by[b, pair, part, high].astype(F32)
                    sm[b, pair, 4 * high + part] = total.astype(BF)

            def give(i):
                other, peer = z_peer(i)
                send(sm.at[b, pair, other], h.at[b, pair, z], rs.at[b, pair], rr.at[b, pair], peer)

            each(1, NZ, give)
            keep(sm.at[b, pair, z], h.at[b, pair, z])

        each(0, 4, step)

    def finish(b):
        each(0, 4, lambda pair: arrived(h.at[b, pair, pl.ds(0, NZ - 1)], rr.at[b, pair]))

        def step(i):
            four = pl.ds(i * 4, 4)
            mixed = jnp.concatenate(
                [
                    (tm[b, pair, four].astype(F32) + h[b, pair, four].astype(F32)).reshape(128, 128)
                    for pair in range(4)
                ],
                axis=1,
            ).astype(BF)
            update = jnp.dot(mixed, wos[...], preferred_element_type=F32)
            out[b, four] = (t_s[b, four].astype(F32) + update.reshape(4, ROWS, D)).astype(BF)

        each(0, 4, step)

    pltpu.make_async_copy(tok.at[0], t_s.at[0], load_sem.at[0]).wait()
    normalize(0)
    pl.semaphore_wait(barrier, 25)
    forward(0)
    pltpu.make_async_copy(tok.at[1], t_s.at[1], load_sem.at[1]).wait()
    normalize(1)
    forward(1)
    for pair in range(4):
        for kind in range(3):
            weight_load(pair, kind).wait()
    time_lines(0)
    time_lines(1)
    for b in range(2):
        spread(b)
        attend(b)
        back(b)
    out_load.wait()
    finish(0)
    finish(1)
    for b in range(2):
        arrived(xn.at[b, pl.ds(0, NZ - 1)], zs.at[b])
        arrived(ry.at[b, pl.ds(0, 3)], ys.at[b])

        @pl.when(core == b)
        def _():
            arrived(r1.at[b, pl.ds(0, 12)], xs.at[b])
            each(0, 4, lambda pair: arrived(ox.at[pair, pl.ds(0, 28)], bxs.at[pair]))

        @pl.when(core != b)
        def _():
            arrived(r1.at[b], xs.at[b])

        def drain(pair):
            arrived(by.at[b, pair, pl.ds(0, 3)], bys.at[b, pair])
            arrived(h.at[b, pair, pl.ds(0, NZ - 1)], rs.at[b, pair])

        each(0, 4, drain)


def body(tokens, norm_gain, w_qkv, w_out):
    shape = tokens.shape
    dma = pltpu.SemaphoreType.DMA
    result = pl.pallas_call(
        kernel,
        out_shape=jax.ShapeDtypeStruct((2, NZ, ROWS, D), BF),
        in_specs=[
            pl.BlockSpec(memory_space=pltpu.HBM),
            pl.BlockSpec(memory_space=pltpu.VMEM),
            pl.BlockSpec(memory_space=pltpu.HBM),
            pl.BlockSpec(memory_space=pltpu.HBM),
        ],
        out_specs=pl.BlockSpec(memory_space=pltpu.VMEM),
        scratch_shapes=[
            pltpu.VMEM((2, NZ, ROWS, D), BF),
            pltpu.VMEM((2, NZ, ROWS, D), BF),
            pltpu.VMEM((2, NZ, ROWS, D), BF),
            pltpu.VMEM((2, 4, 4, ROWS, D), BF),
            pltpu.VMEM((8, 4, ROWS, D), BF),
            pltpu.VMEM((2, 4, NZ, ROWS, 128), BF),
            pltpu.VMEM((4, 32, ROWS, 128), BF),
            pltpu.VMEM((2, 4, 4, 4, ROWS, 128), BF),
            pltpu.VMEM((2, 4, 4, 4, ROWS, 128), BF),
            pltpu.VMEM((2, 4, NZ, ROWS, 128), BF),
            pltpu.VMEM((2, 4, NZ, ROWS, 128), BF),
            pltpu.VMEM((2, 4, NZ, ROWS, 128), BF),
            pltpu.VMEM((3, 1024, 128), F32),
            pltpu.VMEM((1024, 128), F32),
            pltpu.VMEM((8, 256, 128), F32),
            pltpu.VMEM((8, 256, 128), BF),
            pltpu.VMEM((4, 3, D, 128), BF),
            pltpu.VMEM((D, D), BF),
            dma((3,)),
            dma((4, 3)),
            dma,
            dma((2,)),
            dma((2, NZ)),
        ]
        + [dma((2,))] * 4
        + [dma((2, 4)), dma((2, 4)), dma((4,)), dma((2, 4)), dma((2, 4)), dma((2, 4))],
        compiler_params=pltpu.CompilerParams(
            collective_id=0, has_side_effects=True, vmem_limit_bytes=48 * 1024 * 1024
        ),
        name="axial",
    )(tokens.reshape(2, NZ, ROWS, D), norm_gain.reshape(1, D), w_qkv, w_out)
    return result.reshape(shape)


def solution(mesh):
    placed = (P(None, None, "gx", "gy", None), P(), P(), P())
    return jax.shard_map(
        body, mesh=mesh, in_specs=placed, out_specs=P(None, None, "gx", "gy", None), check_vma=False
    )
```

time: 370 us -> 119 us (0.32)
  blocking collectives: 159 us -> 0 us
  Pallas kernels: 0 us -> 114 us
  waiting for transfers between devices: 84.3 us -> 0 us
  local copies, waits for them, and re-layouts: 47.3 us -> 5.33 us
  matrix products: 29.6 us -> 0 us
  starting transfers between devices: 26.9 us -> 0 us
  other arithmetic: 21.3 us -> 0 us
    all_to_all x1 -> x0, blocking collectives: 159 us -> none  [body(): lax.all_to_all(outgoing, 'gy', split_axis=0, concat_axis=2, tiled=True)]
    pallas_call x0 -> x1, Pallas kernels: none -> 114 us  [body(): pl.pallas_call(kernel, out_shape=jax.ShapeDtypeStruct((2, NZ, ROWS, D), B...]
    all_to_all x3 -> x0, waiting for transfers between devices: 84.3 us -> none  [the longest x1 54.6 us: body(): lax.all_to_all(outgoing, 'gx', split_axis=0, concat_axis=1, tiled=True)]
    all_to_all x3 -> x0, starting transfers between devices: 26.9 us -> none  [the longest x1 10.5 us: body(): lax.all_to_all(outcome, 'gx', split_axis=1, concat_axis=0, tiled=True)]
    dot_general x6 -> x0, matrix products: 19.3 us -> none  [the longest x3 8.41 us: attend(): jnp.einsum(form_mix, weights, values, preferred_element_type=jnp.float32)]
    sub x1 -> x0, other arithmetic: 17.7 us -> none  [attend(): expo = jnp.exp(scores - highest)]
    convert_element_type x5 -> x0, local copies, waits for them, and re-layouts: 14 us -> none  [the longest x2 7.97 us: body(): along_time.astype(jnp.float32)]
    slice x6 -> x0, local copies, waits for them, and re-layouts: 12.5 us -> none  [the longest x3 6.02 us: attend(): key_part = triple[..., width:2 * width].reshape(split)]
  transfers between devices with their start and end apart: 3 -> 0, of which waited for: 2 -> 0; matrix products, arithmetic and copies ran while one was open for 24% -> 0% of each run, Pallas kernels for 0% -> 0%
where the time goes in v2:
time: 119 us
  Pallas kernels  114 us (96%)
  local copies, waits for them, and re-layouts  5.33 us (4%)
    pallas_call x1, Pallas kernels, body(): pl.pallas_call(kernel, out_shape=jax.ShapeDtypeStruct((2, NZ, ROWS, D), B...  114 us
    unnamed x9, local copies, waits for them, and re-layouts  5.33 us

profile of v2, /device:TPU:1, one launch (start us, length us, event | category | flops | bytes accessed | tf_op | source)
XLA Modules:
  0.0 118.9 jit_solution(9473976870208219109)
XLA Ops:
  0.0 0.0 copy-start
  0.0 1.4 %copy-done = bf16[512,1536]{1,0:T(8,128)(2,1)S(1)} copy-done((bf16[512,1536]{1,0:T(8,128)(2,1)S(1)}, bf16[512,1536]{1,0:T(8,128)(2,1)}, u32[]{:S(2)}) %copy-start) | copy-done | bytes 1572888
  1.4 0.0 copy-start.1
  1.4 1.2 %copy-done.1 = bf16[2,16,4,8,512]{4,3,2,1,0:T(8,128)(2,1)S(1)} copy-done((bf16[2,16,4,8,512]{4,3,2,1,0:T(8,128)(2,1)S(1)}, bf16[2,16,4,8,512]{4,3,2,1,0:T(8,128)(2,1)}, u32[]{:S(2)}) %copy-start.1) | copy-done | bytes 1048600
  2.6 0.0 copy-start.2
  2.6 1.0 copy-done.2
  3.7 0.0 copy-start.3
  3.7 0.7 copy-done.3
  4.4 113.5 %axial.1 = bf16[2,16,32,512]{3,2,1,0:T(8,128)(2,1)S(1)} custom-call(bf16[2,16,32,512]{3,2,1,0:T(8,128)(2,1)S(1)} %bitcast.4, f32[1,512]{1,0:T(1,128)S(1)} %bitcast.5, bf16[512,1536]{1,0:T(8,128)(2,1)S(1)} %copy-done, bf16[512,512]{1,0:T(8,128)(2,1)S(1)} %copy-done.2), custom_call_target="tpu_custom_call" | custom-call | tf_op jit(solution)/shard_map/axial/pallas_call | solution.py:342
  117.9 1.0 copy.6
Async XLA Ops:
  0.0 1.4 %copy-start = (bf16[512,1536]{1,0:T(8,128)(2,1)S(1)}, bf16[512,1536]{1,0:T(8,128)(2,1)}, u32[]{:S(2)}) copy-start(bf16[512,1536]{1,0:T(8,128)(2,1)} %wq.1) | copy-start | bytes 4718596
  1.4 1.2 %copy-start.1 = (bf16[2,16,4,8,512]{4,3,2,1,0:T(8,128)(2,1)S(1)}, bf16[2,16,4,8,512]{4,3,2,1,0:T(8,128)(2,1)}, u32[]{:S(2)}) copy-start(bf16[2,16,4,8,512]{4,3,2,1,0:T(8,128)(2,1)} %param.4) | copy-start | bytes 3145732
  2.6 1.0 copy-start.2
  3.7 0.7 copy-start.3

commit v3 on v2

--- a/solution.py
+++ b/solution.py
@@ -19,8 +19,8 @@
 
 def kernel(
     tok, gain, wq, wo, out,
-    t_s, xn, r1, ry, rx, oy, ox, by, bx, sm, h, tm, qkv, of, sc, wt, w, wos,
-    load_sem, w_sem, loc_sem, zs, zr, ys, yr, xs, xr, bys, byr, bxs, bxr, rs, rr,
+    t_s, xn, r1, ry, rx, oy, ox, by, bx, sm, h, tm, res, qkv, of, sc, wt, w, wos, gains,
+    load_sem, w_sem, loc_sem, out_sem, near_sem, zs, zr, ys, yr, xs, xr, bys, byr, bxs, bxr, rs, rr,
 ):
     gx, gy = lax.axis_index("gx"), lax.axis_index("gy")
     y, zl, core = gx // 8, (gx // 2) % 4, gx % 2
@@ -28,6 +28,8 @@
     z = zh * 4 + zl
     yc = y * 2 + core
 
+    gain_load = pltpu.make_async_copy(gain, gains, load_sem.at[3])
+    gain_load.start()
     for b in range(2):
         pltpu.make_async_copy(tok.at[b], t_s.at[b], load_sem.at[b]).start()
 
@@ -55,7 +57,7 @@
     def greet(peer):
         return lambda i: pl.semaphore_signal(barrier, inc=1, device_id=peer(i)[1], device_id_type=MESH)
 
-    each(1, NZ, greet(z_peer))
+    each(1, 3, greet(z_peer))
     each(1, 4, greet(x_peer))
     each(1, 8, greet(yc_peer))
 
@@ -69,14 +71,12 @@
             weight_load(pair, kind).start()
     out_load.start()
 
-    scale = gain[...]
-
     def normalize(b):
         def step(i):
             two = pl.ds(i * 2, 2)
             field = t_s[b, two].astype(F32)
             mean = jnp.mean(field * field, axis=-1, keepdims=True)
-            xn[b, two] = (field * lax.rsqrt(mean + 1e-05) * scale).astype(BF)
+            xn[b, two] = (field * lax.rsqrt(mean + 1e-05) * gains[...]).astype(BF)
 
         each(0, NZ // 2, step)
 
@@ -93,13 +93,29 @@
     def arrived(ref, sem):
         pltpu.make_async_copy(ref, ref, sem).wait()
 
-    def forward(b):
-        def step(i):
-            other, peer = z_peer(i)
-            send(xn.at[b, other], r1.at[b, z], zs.at[b], zr.at[b, z], peer)
-
-        each(1, NZ, step)
-        keep(xn.at[b, z], r1.at[b, z])
+    def forward_to(b, i):
+        other, peer = z_peer(i)
+        send(xn.at[b, other], r1.at[b, z], zs.at[b], zr.at[b, z], peer)
+
+    def tell(level):
+        for side in range(2):
+            pl.semaphore_signal(near_sem.at[side, level], inc=1, device_id=z_peer(side + 1)[1], device_id_type=MESH)
+
+    def forward_first():
+        def step(level):
+            tell(level)
+            forward_to(0, 2 * level - 1)
+            forward_to(0, 2 * level)
+            for side in range(2):
+                pl.semaphore_wait(near_sem.at[side, level], 1)
+
+        each(1, 8, step)
+        forward_to(0, 15)
+        keep(xn.at[0, z], r1.at[0, z])
+
+    def forward_second():
+        each(1, NZ, lambda i: forward_to(1, i))
+        keep(xn.at[1, z], r1.at[1, z])
 
     def spread(b):
         def pass_on(other):
@@ -249,36 +265,39 @@
             each(1, 4, give)
             keep(oy.at[b, pair, pl.ds(x * 4, 4)], by.at[b, pair, x])
 
+            @pl.when(pair >= 1)
+            def _():
+                back(b, pair - 1)
+
         each(0, 4, step)
+        back(b, 3)
 
     rx_rows = rx.reshape(32, ROWS, D)
     ry_rows = ry.reshape(2, 16, ROWS, D)
 
-    def back(b):
-        def step(pair):
-            arrived(by.at[b, pair, pl.ds(0, 3)], byr.at[b, pair])
-
-            @pl.when(core == b)
-            def _():
-                arrived(bx.at[b, pair, pl.ds(0, 3)], bxr.at[b, pair])
-
-            @pl.when(core != b)
-            def _():
-                arrived(bx.at[b, pair], bxr.at[b, pair])
-
-            for high in range(4):
-                for part in range(4):
-                    total = bx[b, pair, high, part].astype(F32) + by[b, pair, part, high].astype(F32)
-                    sm[b, pair, 4 * high + part] = total.astype(BF)
-
-            def give(i):
-                other, peer = z_peer(i)
-                send(sm.at[b, pair, other], h.at[b, pair, z], rs.at[b, pair], rr.at[b, pair], peer)
-
-            each(1, NZ, give)
-            keep(sm.at[b, pair, z], h.at[b, pair, z])
-
-        each(0, 4, step)
+    def back(b, pair):
+        arrived(by.at[b, pair, pl.ds(0, 3)], byr.at[b, pair])
+
+        @pl.when(core == b)
+        def _():
+            arrived(bx.at[b, pair, pl.ds(0, 3)], bxr.at[b, pair])
+
+        @pl.when(core != b)
+        def _():
+            arrived(bx.at[b, pair], bxr.at[b, pair])
+
+        for high in range(4):
+            for part in range(4):
+                total = bx[b, pair, high, part].astype(F32) + by[b, pair, part, high].astype(F32)
+                sm[b, pair, 4 * high + part] = total.astype(BF)
+
+        def give(i):
+            other, peer = z_peer(NZ - i)
+            send(sm.at[b, pair, other], h.at[b, pair, z], rs.at[b, pair], rr.at[b, pair], peer)
+
+        each(1, NZ, give)
+        keep(sm.at[b, pair, z], h.at[b, pair, z])
+
 
     def finish(b):
         each(0, 4, lambda pair: arrived(h.at[b, pair, pl.ds(0, NZ - 1)], rr.at[b, pair]))
@@ -293,17 +312,19 @@
                 axis=1,
             ).astype(BF)
             update = jnp.dot(mixed, wos[...], preferred_element_type=F32)
-            out[b, four] = (t_s[b, four].astype(F32) + update.reshape(4, ROWS, D)).astype(BF)
+            res[b, four] = (t_s[b, four].astype(F32) + update.reshape(4, ROWS, D)).astype(BF)
+            pltpu.make_async_copy(res.at[b, four], out.at[b, four], out_sem.at[b]).start()
 
         each(0, 4, step)
 
     pltpu.make_async_copy(tok.at[0], t_s.at[0], load_sem.at[0]).wait()
+    gain_load.wait()
     normalize(0)
-    pl.semaphore_wait(barrier, 25)
-    forward(0)
+    pl.semaphore_wait(barrier, 12)
+    forward_first()
     pltpu.make_async_copy(tok.at[1], t_s.at[1], load_sem.at[1]).wait()
     normalize(1)
-    forward(1)
+    forward_second()
     for pair in range(4):
         for kind in range(3):
             weight_load(pair, kind).wait()
@@ -312,7 +333,6 @@
     for b in range(2):
         spread(b)
         attend(b)
-        back(b)
     out_load.wait()
     finish(0)
     finish(1)
@@ -334,6 +354,7 @@
             arrived(h.at[b, pair, pl.ds(0, NZ - 1)], rs.at[b, pair])
 
         each(0, 4, drain)
+        pltpu.make_async_copy(res.at[b], out.at[b], out_sem.at[b]).wait()
 
 
 def body(tokens, norm_gain, w_qkv, w_out):
@@ -343,12 +364,12 @@
         kernel,
         out_shape=jax.ShapeDtypeStruct((2, NZ, ROWS, D), BF),
         in_specs=[
-            pl.BlockSpec(memory_space=pltpu.HBM),
-            pl.BlockSpec(memory_space=pltpu.VMEM),
-            pl.BlockSpec(memory_space=pltpu.HBM),
-            pl.BlockSpec(memory_space=pltpu.HBM),
+            pl.BlockSpec(memory_space=pl.ANY),
+            pl.BlockSpec(memory_space=pl.ANY),
+            pl.BlockSpec(memory_space=pl.ANY),
+            pl.BlockSpec(memory_space=pl.ANY),
         ],
-        out_specs=pl.BlockSpec(memory_space=pltpu.VMEM),
+        out_specs=pl.BlockSpec(memory_space=pl.ANY),
         scratch_shapes=[
             pltpu.VMEM((2, NZ, ROWS, D), BF),
             pltpu.VMEM((2, NZ, ROWS, D), BF),
@@ -362,22 +383,26 @@
             pltpu.VMEM((2, 4, NZ, ROWS, 128), BF),
             pltpu.VMEM((2, 4, NZ, ROWS, 128), BF),
             pltpu.VMEM((2, 4, NZ, ROWS, 128), BF),
+            pltpu.VMEM((2, NZ, ROWS, D), BF),
             pltpu.VMEM((3, 1024, 128), F32),
             pltpu.VMEM((1024, 128), F32),
             pltpu.VMEM((8, 256, 128), F32),
             pltpu.VMEM((8, 256, 128), BF),
             pltpu.VMEM((4, 3, D, 128), BF),
             pltpu.VMEM((D, D), BF),
-            dma((3,)),
+            pltpu.VMEM((1, D), F32),
+            dma((4,)),
             dma((4, 3)),
             dma,
+            dma((2,)),
+            pltpu.SemaphoreType.REGULAR((2, 8)),
             dma((2,)),
             dma((2, NZ)),
         ]
         + [dma((2,))] * 4
         + [dma((2, 4)), dma((2, 4)), dma((4,)), dma((2, 4)), dma((2, 4)), dma((2, 4))],
         compiler_params=pltpu.CompilerParams(
-            collective_id=0, has_side_effects=True, vmem_limit_bytes=48 * 1024 * 1024
+            collective_id=0, has_side_effects=True, vmem_limit_bytes=67043328
         ),
         name="axial",
     )(tokens.reshape(2, NZ, ROWS, D), norm_gain.reshape(1, D), w_qkv, w_out)

time: 119 us -> 113 us (0.950)
  Pallas kernels: 114 us -> 110 us
  local copies, waits for them, and re-layouts: 5.33 us -> 2.3 us
    pallas_call x1, Pallas kernels: 114 us -> 110 us  [body(): pl.pallas_call(kernel, out_shape=jax.ShapeDtypeStruct((2, NZ, ROWS, D), B...]
    unnamed x9 -> x1, local copies, waits for them, and re-layouts: 5.33 us -> 2.3 us
where the time goes in v3:
time: 113 us
  Pallas kernels  110 us (97%)
  local copies, waits for them, and re-layouts  2.3 us (2%)
    pallas_call x1, Pallas kernels, body(): pl.pallas_call(kernel, out_shape=jax.ShapeDtypeStruct((2, NZ, ROWS, D), B...  110 us
    unnamed x1, local copies, waits for them, and re-layouts  2.3 us

profile of v3, /device:TPU:1, one launch (start us, length us, event | category | flops | bytes accessed | tf_op | source)
XLA Modules:
  0.0 112.7 jit_solution(10163925984553155003)
XLA Ops:
  0.0 110.4 %axial.1 = bf16[2,16,32,512]{3,2,1,0:T(8,128)(2,1)} custom-call(bf16[2,16,32,512]{3,2,1,0:T(8,128)(2,1)} %bitcast.4, f32[1,512]{1,0:T(1,128)} %bitcast.5, bf16[512,1536]{1,0:T(8,128)(2,1)} %wq.1, bf16[512,512]{1,0:T(8,128)(2,1)} %wo.1), custom_call_target="tpu_custom_call" | custom-call | tf_op jit(solution)/shard_map/axial/pallas_call | solution.py:363
  110.4 2.3 %copy.6 = bf16[2,16,4,8,512]{4,3,2,1,0:T(8,128)(2,1)} copy(bf16[2,16,4,8,512]{4,3,2,1,0:T(8,128)(2,1)} %bitcast.3) | data formatting | bytes 2097152

commit v4 on v3

--- a/solution.py
+++ b/solution.py
@@ -19,8 +19,8 @@
 
 def kernel(
     tok, gain, wq, wo, out,
-    t_s, xn, r1, ry, rx, oy, ox, by, bx, sm, h, tm, res, qkv, of, sc, wt, w, wos, gains,
-    load_sem, w_sem, loc_sem, out_sem, near_sem, zs, zr, ys, yr, xs, xr, bys, byr, bxs, bxr, rs, rr,
+    t_s, xn, r1, ry, rx, oy, ox, by, bx, sm, h, tm, qkv, of, sc, wt, w, wos, gains,
+    load_sem, w_sem, loc_sem, near_sem, zs, zr, ys, yr, xs, xr, bys, byr, bxs, bxr, rs, rr,
 ):
     gx, gy = lax.axis_index("gx"), lax.axis_index("gy")
     y, zl, core = gx // 8, (gx // 2) % 4, gx % 2
@@ -312,8 +312,7 @@
                 axis=1,
             ).astype(BF)
             update = jnp.dot(mixed, wos[...], preferred_element_type=F32)
-            res[b, four] = (t_s[b, four].astype(F32) + update.reshape(4, ROWS, D)).astype(BF)
-            pltpu.make_async_copy(res.at[b, four], out.at[b, four], out_sem.at[b]).start()
+            out[b, four] = (t_s[b, four].astype(F32) + update.reshape(4, ROWS, D)).astype(BF)
 
         each(0, 4, step)
 
@@ -354,12 +353,12 @@
             arrived(h.at[b, pair, pl.ds(0, NZ - 1)], rs.at[b, pair])
 
         each(0, 4, drain)
-        pltpu.make_async_copy(res.at[b], out.at[b], out_sem.at[b]).wait()
 
 
 def body(tokens, norm_gain, w_qkv, w_out):
     shape = tokens.shape
     dma = pltpu.SemaphoreType.DMA
+    operands = (tokens.reshape(2, NZ, ROWS, D), norm_gain.reshape(1, D), w_qkv, w_out)
     result = pl.pallas_call(
         kernel,
         out_shape=jax.ShapeDtypeStruct((2, NZ, ROWS, D), BF),
@@ -369,7 +368,7 @@
             pl.BlockSpec(memory_space=pl.ANY),
             pl.BlockSpec(memory_space=pl.ANY),
         ],
-        out_specs=pl.BlockSpec(memory_space=pl.ANY),
+        out_specs=pl.BlockSpec(memory_space=pltpu.VMEM),
         scratch_shapes=[
             pltpu.VMEM((2, NZ, ROWS, D), BF),
             pltpu.VMEM((2, NZ, ROWS, D), BF),
@@ -383,7 +382,6 @@
             pltpu.VMEM((2, 4, NZ, ROWS, 128), BF),
             pltpu.VMEM((2, 4, NZ, ROWS, 128), BF),
             pltpu.VMEM((2, 4, NZ, ROWS, 128), BF),
-            pltpu.VMEM((2, NZ, ROWS, D), BF),
             pltpu.VMEM((3, 1024, 128), F32),
             pltpu.VMEM((1024, 128), F32),
             pltpu.VMEM((8, 256, 128), F32),
@@ -394,7 +392,6 @@
             dma((4,)),
             dma((4, 3)),
             dma,
-            dma((2,)),
             pltpu.SemaphoreType.REGULAR((2, 8)),
             dma((2,)),
             dma((2, NZ)),
@@ -402,10 +399,10 @@
         + [dma((2,))] * 4
         + [dma((2, 4)), dma((2, 4)), dma((4,)), dma((2, 4)), dma((2, 4)), dma((2, 4))],
         compiler_params=pltpu.CompilerParams(
-            collective_id=0, has_side_effects=True, vmem_limit_bytes=67043328
+            collective_id=0, has_side_effects=True, vmem_limit_bytes=48 * 1024 * 1024
         ),
         name="axial",
-    )(tokens.reshape(2, NZ, ROWS, D), norm_gain.reshape(1, D), w_qkv, w_out)
+    )(*(pltpu.with_memory_space_constraint(a, pltpu.HBM) for a in operands))
     return result.reshape(shape)
 
 

time: 113 us -> 111 us (0.982)
  local copies, waits for them, and re-layouts: 2.3 us -> 0.97 us
    unnamed x1, local copies, waits for them, and re-layouts: 2.3 us -> 0.97 us
where the time goes in v4:
time: 111 us
  Pallas kernels  110 us (99%)
    pallas_call x1, Pallas kernels, body(): pl.pallas_call(kernel, out_shape=jax.ShapeDtypeStruct((2, NZ, ROWS, D), B...  110 us

profile of v4, /device:TPU:1, one launch (start us, length us, event | category | flops | bytes accessed | tf_op | source)
XLA Modules:
  0.0 110.8 jit_solution(16092038724974837471)
XLA Ops:
  0.0 109.8 %axial.1 = bf16[2,16,32,512]{3,2,1,0:T(8,128)(2,1)S(1)} custom-call(bf16[2,16,32,512]{3,2,1,0:T(8,128)(2,1)} %bitcast.4, f32[1,512]{1,0:T(1,128)} %bitcast.5, bf16[512,1536]{1,0:T(8,128)(2,1)} %wq.1, bf16[512,512]{1,0:T(8,128)(2,1)} %wo.1), custom_call_target="tpu_custom_call" | custom-call | tf_op jit(solution)/shard_map/axial/pallas_call | solution.py:362
  109.8 1.0 copy.6

commit v5 on v4

--- a/solution.py
+++ b/solution.py
@@ -323,12 +323,12 @@
     forward_first()
     pltpu.make_async_copy(tok.at[1], t_s.at[1], load_sem.at[1]).wait()
     normalize(1)
-    forward_second()
     for pair in range(4):
         for kind in range(3):
             weight_load(pair, kind).wait()
     time_lines(0)
     time_lines(1)
+    forward_second()
     for b in range(2):
         spread(b)
         attend(b)

time: 111 us -> 111 us (level)
  no operation moved by 1% of the time
where the time goes in v5:
time: 111 us; the launch traced here: 110 us
  Pallas kernels  109 us (98%)
    pallas_call x1, Pallas kernels, body(): pl.pallas_call(kernel, out_shape=jax.ShapeDtypeStruct((2, NZ, ROWS, D), B...  109 us

profile of v5, /device:TPU:1, one launch (start us, length us, event | category | flops | bytes accessed | tf_op | source)
XLA Modules:
  0.0 110.3 jit_solution(3014444171840190966)
XLA Ops:
  0.0 109.4 %axial.1 = bf16[2,16,32,512]{3,2,1,0:T(8,128)(2,1)S(1)} custom-call(bf16[2,16,32,512]{3,2,1,0:T(8,128)(2,1)} %bitcast.4, f32[1,512]{1,0:T(1,128)} %bitcast.5, bf16[512,1536]{1,0:T(8,128)(2,1)} %wq.1, bf16[512,512]{1,0:T(8,128)(2,1)} %wo.1), custom_call_target="tpu_custom_call" | custom-call | tf_op jit(solution)/shard_map/axial/pallas_call | solution.py:362
  109.4 1.0 copy.6
